TPU v7x, 32 devices: a whole 2x2x4 slice. The times are simulated.
32 devices in a mesh: sub: 8 (over y, x, core), grp: 4 (over z).
Axes of the slice: x: 2, y: 2, z: 4, core: 2. Of those that a mesh axis runs over, the one named last changes fastest.
Arguments:
- res_inner: bfloat16 [2048, 16, 144], P(('sub', 'grp')), may hold values from -6 to 6
- res_face: bfloat16 [1024, 16, 144], P(('sub', 'grp')), may hold values from -6 to 6
- inner_inv: bfloat16 [2048, 144, 144], P(('sub', 'grp')), may hold values from -0.5 to 0.5
- face_coupling: bfloat16 [1024, 144, 144], P(('sub', 'grp')), may hold values from -0.5 to 0.5
- face_elem: int32 [32, 32], P(('sub', 'grp')), may hold values from 0 to 63
- face_inv: bfloat16 [1024, 144, 144], P(('sub', 'grp')), may hold values from -0.5 to 0.5
- coarse_basis: bfloat16 [1024, 64, 144], P(('sub', 'grp')), may hold values from -0.0625 to 0.0625
- coarse_map: int32 [32, 64], P(('sub', 'grp')), may hold values from 0 to 511
- coarse_inv: float32 [512, 512], P('grp'), as said below
- recv_index: int32 [32, 32], P(('sub', 'grp')), may hold values from 0 to 8, as said below
- sharers: int32 [32, 32], P(('sub', 'grp')), may hold values from 0 to 32, as said below
Outputs:
- inner_out: bfloat16 [2048, 16, 144], P(('sub', 'grp'))
- face_out: bfloat16 [1024, 16, 144], P(('sub', 'grp'))
Inputs may be any that keep to these rules, and one draw needn't show every extreme that they name: `recv_index`: row o gives, for each subdomain s at position s, the index among the 8 blocks owned by subdomain o that slot o of subdomain s refers to, or 8 where that slot is unused. `sharers`: for a used slot, the number of used slots of all subdomains that refer to the same owned block, up to all 32 of them, which some block reaches; 0 exactly for unused slots. coarse_inv is symmetric.
All inputs are finite; a program needn't handle non-finite values.
Results may differ from a plain program's by a relative error of at most 0.006.
Values may be sent and summed in bfloat16 or wider, within the bound.
No kernel may reach another device: no remote copies, remote signals or barrier semaphores. Data moves between devices by JAX's collectives and lax.ppermute only.
A program may use at most 128 MiB of HBM per device.

v0:
```python
import jax
import jax.numpy as jnp
from jax import lax
from jax.sharding import PartitionSpec as P


def send_out(partials):
    return lax.all_to_all(partials, ("sub", "grp"), split_axis=0, concat_axis=0, tiled=True)


def send_back(spread):
    return lax.all_to_all(spread, ("sub", "grp"), split_axis=0, concat_axis=0, tiled=True)


def body(
    res_inner,
    res_face,
    inner_inv,
    face_coupling,
    face_elem,
    face_inv,
    coarse_basis,
    coarse_map,
    coarse_inv,
    recv_index,
    sharers,
):
    num_faces = res_face.shape[0]
    num_owned = num_faces // 4
    elements = res_inner.shape[0]
    num_coarse = coarse_inv.shape[1]
    counts = sharers[0]
    weights = jnp.where(counts > 0, 1.0 / jnp.maximum(counts, 1).astype(jnp.float32), 0.0)
    owner_onehot = (
        recv_index[0][None, :] == jnp.arange(num_owned, dtype=jnp.int32)[:, None]
    ).astype(jnp.bfloat16)

    def assemble(partials):
        received = send_out(partials)
        flattened = received.reshape(num_faces, -1)
        owner_sum = jnp.dot(owner_onehot, flattened, preferred_element_type=jnp.float32).astype(
            jnp.bfloat16
        )
        spread = jnp.einsum(
            "of,ok->fk", owner_onehot, owner_sum, preferred_element_type=jnp.float32
        ).astype(jnp.bfloat16)
        return send_back(spread.reshape(partials.shape))

    inner_w = jnp.einsum(
        "erb,ecb->erc", res_inner, inner_inv, preferred_element_type=jnp.float32
    ).astype(jnp.bfloat16)
    nearby = inner_w[face_elem[0]]
    condensed = res_face.astype(jnp.float32) - jnp.einsum(
        "lrb,lcb->lrc", nearby, face_coupling, preferred_element_type=jnp.float32
    )
    sent = (weights[:, None, None] * condensed).astype(jnp.bfloat16)
    gathered = assemble(sent)
    restricted = (weights[:, None, None] * gathered.astype(jnp.float32)).astype(jnp.bfloat16)
    local_coarse = jnp.einsum(
        "ljb,lrb->jr", coarse_basis, restricted, preferred_element_type=jnp.float32
    )
    coarse_onehot = (
        coarse_map[0][None, :] == jnp.arange(num_coarse, dtype=jnp.int32)[:, None]
    ).astype(jnp.float32)
    partial_rhs = jnp.dot(coarse_onehot, local_coarse, precision=lax.Precision.HIGHEST)
    coarse_rhs = lax.psum(partial_rhs, ("sub", "grp"))
    row_part = jnp.dot(coarse_inv, coarse_rhs, precision=lax.Precision.HIGHEST)
    coarse_sol = lax.all_gather(row_part, "grp", axis=0, tiled=True)
    picked = jnp.einsum(
        "kj,kr->jr", coarse_onehot, coarse_sol, precision=lax.Precision.HIGHEST
    ).astype(jnp.bfloat16)
    coarse_part = jnp.einsum(
        "ljb,jr->lrb", coarse_basis, picked, preferred_element_type=jnp.float32
    )
    local_part = jnp.einsum(
        "lrb,lcb->lrc", restricted, face_inv, preferred_element_type=jnp.float32
    )
    weighted = (weights[:, None, None] * (coarse_part + local_part)).astype(jnp.bfloat16)
    face_out = assemble(weighted)
    contrib = jnp.einsum(
        "lrc,lcb->lrb", face_out, face_coupling, preferred_element_type=jnp.float32
    )
    elem_onehot = (face_elem[0][None, :] == jnp.arange(elements, dtype=jnp.int32)[:, None]).astype(
        jnp.float32
    )
    scattered = jnp.dot(
        elem_onehot, contrib.reshape(num_faces, -1), precision=lax.Precision.HIGHEST
    ).reshape(res_inner.shape)
    inner_rhs = (res_inner.astype(jnp.float32) - scattered).astype(jnp.bfloat16)
    inner_out = jnp.einsum(
        "erb,ecb->erc", inner_rhs, inner_inv, preferred_element_type=jnp.float32
    ).astype(jnp.bfloat16)
    return (inner_out, face_out)


def solution(mesh):
    return jax.shard_map(
        body,
        mesh=mesh,
        in_specs=(
            P(("sub", "grp"), None, None),
            P(("sub", "grp"), None, None),
            P(("sub", "grp"), None, None),
            P(("sub", "grp"), None, None),
            P(("sub", "grp"), None),
            P(("sub", "grp"), None, None),
            P(("sub", "grp"), None, None),
            P(("sub", "grp"), None),
            P("grp", None),
            P(("sub", "grp"), None),
            P(("sub", "grp"), None),
        ),
        out_specs=(P(("sub", "grp"), None, None), P(("sub", "grp"), None, None)),
        check_vma=False,
    )
```

profile of v0, /device:TPU:0, one launch (start us, length us, event | category | flops | bytes accessed | tf_op | source)
XLA Modules:
  0.0 140.8 jit_solution(13594599169915256372)
XLA Ops:
  0.6 0.0 copy-start
  0.6 0.8 fusion.20
  1.5 0.7 fusion.19
  2.1 3.8 %convolution_convert_fusion.5 = bf16[64,16,144]{2,1,0:T(8,128)(2,1)S(1)} fusion(bf16[64,16,144]{2,1,0:T(8,128)(2,1)} %param.11, bf16[64,144,144]{2,1,0:T(8,128)(2,1)} %param.13), kind=kOutput, calls=%fused_computation.6 | convolution fusion | flops 42614784 | bytes 3244032 | tf_op jit(solution)/shard_map/erb,ecb->erc/dot_general | solution.py:49
  6.0 1.3 gather_fusion
  7.3 1.8 %fusion.2 = bf16[32,16,144]{2,1,0:T(8,128)(2,1)S(1)} fusion(bf16[32,16,144]{2,1,0:T(8,128)(2,1)} %gather_fusion, bf16[32,144,144]{2,1,0:T(8,128)(2,1)S(1)} %copy-done, bf16[32,16,144]{2,1,0:T(8,128)(2,1)} %param.12, f32[32]{0:T(128)S(1)} %fusion.20), kind=kOutput, calls=%fused_computation.12 | convolution fusion | flops 21528576 | bytes 1769600 | tf_op jit(solution)/shard_map/lrb,lcb->lrc/dot_general | solution.py:53
  9.1 17.5 %all_to_all.20 = bf16[32,16,144]{2,1,0:T(8,128)(2,1)} all-to-all(bf16[32,16,144]{2,1,0:T(8,128)(2,1)S(1)} %fusion.2), channel_id=1, replica_groups=mesh['sub'=8,'grp'=4] {'sub','grp'}, dimensions={0} | all-to-all | bytes 294912 | tf_op jit(solution)/shard_map/all_to_all | solution.py:8
  26.6 1.3 reshape.70
  27.9 1.7 %convolution_convert_fusion.1 = bf16[32,2304]{1,0:T(8,128)(2,1)} fusion(bf16[32,2304]{1,0:T(8,128)(2,1)S(1)} %reshape.70, s32[32]{0:T(128)} %bitcast.41), kind=kOutput, calls=%fused_computation.2 | convolution fusion | flops 2451968 | bytes 295040 | tf_op jit(solution)/shard_map/of,ok->fk/dot_general | solution.py:44
  29.5 2.0 %reshape.71 = bf16[32,16,144]{2,1,0:T(8,128)(2,1)} reshape(bf16[32,2304]{1,0:T(8,128)(2,1)} %convolution_convert_fusion.1) | data formatting | bytes 294912 | tf_op jit(solution)/shard_map/reshape | solution.py:47
  31.6 12.9 %all_to_all.21 = bf16[32,16,144]{2,1,0:T(8,128)(2,1)S(1)} all-to-all(bf16[32,16,144]{2,1,0:T(8,128)(2,1)} %reshape.71), channel_id=1, replica_groups=mesh['sub'=8,'grp'=4] {'sub','grp'}, dimensions={0} | all-to-all | bytes 294912 | tf_op jit(solution)/shard_map/all_to_all | solution.py:12
  44.5 0.7 copy-done.2
  45.2 1.1 convolution_bitcast_fusion.1
  46.3 1.6 %fusion.9 = f32[512,16]{1,0:T(8,128)} fusion(f32[16,64]{1,0:T(8,128)S(1)} %convolution_bitcast_fusion.1, s32[64]{0:T(128)} %bitcast.43), kind=kOutput, calls=%fused_computation.24 | convolution fusion | flops 6324224 | bytes 37120 | tf_op jit(solution)/shard_map/dot_general | solution.py:65
  47.9 41.1 %psum.7 = f32[512,16]{1,0:T(8,128)} all-reduce(f32[512,16]{1,0:T(8,128)} %fusion.9), channel_id=1, replica_groups=mesh['sub'=8,'grp'=4] {'sub','grp'}, use_global_device_ids=true, to_apply=%region_0.1 | all-reduce | flops 8192 | bytes 65536 | tf_op jit(solution)/shard_map/psum | solution.py:66
  89.0 1.6 %convolution_bitcast_fusion.2 = f32[128,16]{0,1:T(8,128)S(1)} fusion(f32[512,16]{1,0:T(8,128)} %psum.7, f32[128,512]{1,0:T(8,128)} %param.19), kind=kOutput, calls=%fused_computation.15 | convolution fusion | flops 12582912 | bytes 303104 | tf_op jit(solution)/shard_map/dot_general | solution.py:67
  90.7 13.1 %all_gather.3 = f32[512,16]{0,1:T(8,128)S(1)} all-gather(f32[128,16]{0,1:T(8,128)S(1)} %convolution_bitcast_fusion.2), channel_id=1, replica_groups=mesh['sub'=8,'grp'=4] {'grp'}, dimensions={0}, use_global_device_ids=true | all-gather | bytes 40960 | tf_op jit(solution)/shard_map/all_gather | solution.py:68
  103.8 0.2 fusion.4
  104.0 0.3 convolution_bitcast_fusion
  104.3 0.0 copy-start.4
  104.3 2.4 %fusion.3 = bf16[32,16,144]{2,1,0:T(8,128)(2,1)S(1)} fusion(f32[32,16,144]{2,1,0:T(8,128)S(1)} %convolution_bitcast_fusion, bf16[32,144,144]{2,1,0:T(8,128)(2,1)} %param.16, f32[32]{0:T(128)S(1)} %copy-done.6, bf16[32,16,144]{2,1,0:T(8,128)(2,1)S(1)} %copy-done.3), kind=kOutput, calls=%fused_computation.13 | convolution fusion | flops 21676032 | bytes 1917056 | tf_op jit(solution)/shard_map/lrb,lcb->lrc/dot_general | solution.py:75
  106.7 13.0 %all_to_all.22 = bf16[32,16,144]{2,1,0:T(8,128)(2,1)S(1)} all-to-all(bf16[32,16,144]{2,1,0:T(8,128)(2,1)S(1)} %fusion.3), channel_id=1, replica_groups=mesh['sub'=8,'grp'=4] {'sub','grp'}, dimensions={0} | all-to-all | bytes 294912 | tf_op jit(solution)/shard_map/all_to_all | solution.py:8
  119.7 0.3 reshape.72
  120.0 0.3 convolution_convert_fusion
  120.3 0.4 reshape.73
  120.7 12.7 %all_to_all.23 = bf16[32,16,144]{2,1,0:T(8,128)(2,1)S(1)} all-to-all(bf16[32,16,144]{2,1,0:T(8,128)(2,1)S(1)} %reshape.73), channel_id=1, replica_groups=mesh['sub'=8,'grp'=4] {'sub','grp'}, dimensions={0} | all-to-all | bytes 294912 | tf_op jit(solution)/shard_map/all_to_all | solution.py:12
  133.4 0.4 fusion.21
  133.8 0.3 reshape.74
  134.1 0.4 dot_general.66
  134.5 0.9 fusion.7
  135.4 4.7 %convolution_convert_fusion.4 = bf16[64,16,144]{2,1,0:T(8,128)(2,1)} fusion(bf16[64,144,144]{2,1,0:T(8,128)(2,1)} %param.13, f32[64,16,144]{2,0,1:T(8,128)S(1)} %fusion.7, bf16[64,16,144]{2,1,0:T(8,128)(2,1)} %param.11), kind=kOutput, calls=%fused_computation.5 | convolution fusion | flops 43057152 | bytes 3833856 | tf_op jit(solution)/shard_map/erb,ecb->erc/dot_general | solution.py:90
  140.1 0.7 copy.22
  (16 shorter events, 0.0 us)
Async XLA Ops:
  0.6 6.6 %copy-start = (bf16[32,144,144]{2,1,0:T(8,128)(2,1)S(1)}, bf16[32,144,144]{2,1,0:T(8,128)(2,1)}, u32[]{:S(2)}) copy-start(bf16[32,144,144]{2,1,0:T(8,128)(2,1)} %param.14) | copy-start | bytes 3981316
  1.5 5.8 %copy-start.5 = (f32[32]{0:T(128)}, f32[32]{0:T(128)S(1)}, u32[]{:S(2)}) copy-start(f32[32]{0:T(128)S(1)} %fusion.20) | copy-start | bytes 388
  7.3 38.0 %copy-start.1 = (bf16[32,64,144]{2,1,0:T(8,128)(2,1)S(1)}, bf16[32,64,144]{2,1,0:T(8,128)(2,1)}, u32[]{:S(2)}) copy-start(bf16[32,64,144]{2,1,0:T(8,128)(2,1)} %param.17) | copy-start | bytes 1769476
  29.5 74.3 %copy-start.7 = (s32[1,64]{1,0:T(1,128)S(1)}, s32[1,64]{1,0:T(1,128)}, u32[]{:S(2)}) copy-start(s32[1,64]{1,0:T(1,128)} %param.18) | copy-start | bytes 772
  31.6 72.7 %copy-start.6 = (f32[32]{0:T(128)S(1)}, f32[32]{0:T(128)}, u32[]{:S(2)}) copy-start(f32[32]{0:T(128)} %copy-done.5) | copy-start | bytes 388
  44.5 0.7 copy-start.2
  89.0 15.2 %copy-start.3 = (bf16[32,16,144]{2,1,0:T(8,128)(2,1)S(1)}, bf16[32,16,144]{2,1,0:T(8,128)(2,1)}, u32[]{:S(2)}) copy-start(bf16[32,16,144]{2,1,0:T(8,128)(2,1)} %copy-done.2) | copy-start | bytes 442372
  104.3 15.7 %copy-start.4 = (s32[1,32]{1,0:T(1,128)S(1)}, s32[1,32]{1,0:T(1,128)}, u32[]{:S(2)}) copy-start(s32[1,32]{1,0:T(1,128)} %param.20) | copy-start | bytes 388
  133.4 1.1 copy-start.8
where the time goes:
time: 141 us
  blocking collectives  110 us (78%)
  matrix products  20.8 us (15%)
  local copies, waits for them, and re-layouts  7.45 us (5%)
  other arithmetic  1.48 us (1%)
    psum x1, blocking collectives, body(): coarse_rhs = lax.psum(partial_rhs, ('sub', 'grp'))  41.1 us
    all_to_all x2, blocking collectives, send_out(): lax.all_to_all(partials, ('sub', 'grp'), split_axis=0, concat_axis=0, til...  30.4 us
    all_to_all x2, blocking collectives, send_back(): lax.all_to_all(spread, ('sub', 'grp'), split_axis=0, concat_axis=0, tiled...  25.6 us
    all_gather x1, blocking collectives, body(): coarse_sol = lax.all_gather(row_part, 'grp', axis=0, tiled=True)  13.1 us
    dot_general x1, matrix products, body(): jnp.einsum('erb,ecb->erc', inner_rhs, inner_inv, preferred_element_type=j...  4.68 us
    dot_general x1, matrix products, body(): jnp.einsum('erb,ecb->erc', res_inner, inner_inv, preferred_element_type=j...  3.82 us

commit v1 on v0

--- a/solution.py
+++ b/solution.py
@@ -63,7 +63,7 @@
         coarse_map[0][None, :] == jnp.arange(num_coarse, dtype=jnp.int32)[:, None]
     ).astype(jnp.float32)
     partial_rhs = jnp.dot(coarse_onehot, local_coarse, precision=lax.Precision.HIGHEST)
-    coarse_rhs = lax.psum(partial_rhs, ("sub", "grp"))
+    coarse_rhs = lax.psum(lax.psum(partial_rhs, "grp"), "sub")
     row_part = jnp.dot(coarse_inv, coarse_rhs, precision=lax.Precision.HIGHEST)
     coarse_sol = lax.all_gather(row_part, "grp", axis=0, tiled=True)
     picked = jnp.einsum(

time: 141 us -> 149 us (1.057)
  blocking collectives: 110 us -> 117 us
    psum x1 -> x2, blocking collectives: 41.1 us -> 49.2 us  [body(): coarse_rhs = lax.psum(lax.psum(partial_rhs, 'grp'), 'sub')]
where the time goes in v1:
time: 149 us; the launch traced here: 148 us
  blocking collectives  117 us (79%)
  matrix products  20.9 us (14%)
  local copies, waits for them, and re-layouts  7.45 us (5%)
    psum x2, blocking collectives, body(): coarse_rhs = lax.psum(lax.psum(partial_rhs, 'grp'), 'sub')  49.2 us
    all_to_all x2, blocking collectives, send_out(): lax.all_to_all(partials, ('sub', 'grp'), split_axis=0, concat_axis=0, til...  29.4 us
    all_to_all x2, blocking collectives, send_back(): lax.all_to_all(spread, ('sub', 'grp'), split_axis=0, concat_axis=0, tiled...  25.6 us
    all_gather x1, blocking collectives, body(): coarse_sol = lax.all_gather(row_part, 'grp', axis=0, tiled=True)  13.1 us
    dot_general x1, matrix products, body(): jnp.einsum('erb,ecb->erc', inner_rhs, inner_inv, preferred_element_type=j...  4.68 us
    dot_general x1, matrix products, body(): jnp.einsum('erb,ecb->erc', res_inner, inner_inv, preferred_element_type=j...  3.82 us

profile of v1, /device:TPU:0, one launch (start us, length us, event | category | flops | bytes accessed | tf_op | source)
XLA Modules:
  0.0 147.9 jit_solution(3697326808426598922)
XLA Ops:
  0.6 0.0 copy-start
  0.6 0.8 fusion.20
  1.5 0.7 fusion.19
  2.1 3.8 %convolution_convert_fusion.5 = bf16[64,16,144]{2,1,0:T(8,128)(2,1)S(1)} fusion(bf16[64,16,144]{2,1,0:T(8,128)(2,1)} %param.11, bf16[64,144,144]{2,1,0:T(8,128)(2,1)} %param.13), kind=kOutput, calls=%fused_computation.6 | convolution fusion | flops 42614784 | bytes 3244032 | tf_op jit(solution)/shard_map/erb,ecb->erc/dot_general | solution.py:49
  6.0 1.3 gather_fusion
  7.3 1.8 %fusion.2 = bf16[32,16,144]{2,1,0:T(8,128)(2,1)S(1)} fusion(bf16[32,16,144]{2,1,0:T(8,128)(2,1)} %gather_fusion, bf16[32,144,144]{2,1,0:T(8,128)(2,1)S(1)} %copy-done, bf16[32,16,144]{2,1,0:T(8,128)(2,1)} %param.12, f32[32]{0:T(128)S(1)} %fusion.20), kind=kOutput, calls=%fused_computation.12 | convolution fusion | flops 21528576 | bytes 1769600 | tf_op jit(solution)/shard_map/lrb,lcb->lrc/dot_general | solution.py:53
  9.1 17.5 %all_to_all.20 = bf16[32,16,144]{2,1,0:T(8,128)(2,1)} all-to-all(bf16[32,16,144]{2,1,0:T(8,128)(2,1)S(1)} %fusion.2), channel_id=1, replica_groups=mesh['sub'=8,'grp'=4] {'sub','grp'}, dimensions={0} | all-to-all | bytes 294912 | tf_op jit(solution)/shard_map/all_to_all | solution.py:8
  26.6 1.3 reshape.70
  27.9 1.7 %convolution_convert_fusion.1 = bf16[32,2304]{1,0:T(8,128)(2,1)} fusion(bf16[32,2304]{1,0:T(8,128)(2,1)S(1)} %reshape.70, s32[32]{0:T(128)} %bitcast.41), kind=kOutput, calls=%fused_computation.2 | convolution fusion | flops 2451968 | bytes 295040 | tf_op jit(solution)/shard_map/of,ok->fk/dot_general | solution.py:44
  29.5 2.0 %reshape.71 = bf16[32,16,144]{2,1,0:T(8,128)(2,1)} reshape(bf16[32,2304]{1,0:T(8,128)(2,1)} %convolution_convert_fusion.1) | data formatting | bytes 294912 | tf_op jit(solution)/shard_map/reshape | solution.py:47
  31.6 12.9 %all_to_all.21 = bf16[32,16,144]{2,1,0:T(8,128)(2,1)S(1)} all-to-all(bf16[32,16,144]{2,1,0:T(8,128)(2,1)} %reshape.71), channel_id=1, replica_groups=mesh['sub'=8,'grp'=4] {'sub','grp'}, dimensions={0} | all-to-all | bytes 294912 | tf_op jit(solution)/shard_map/all_to_all | solution.py:12
  44.5 0.7 copy-done.2
  45.2 1.2 convolution_bitcast_fusion.1
  46.4 1.6 %fusion.9 = f32[512,16]{1,0:T(8,128)} fusion(f32[16,64]{1,0:T(8,128)S(1)} %convolution_bitcast_fusion.1, s32[64]{0:T(128)} %bitcast.43), kind=kOutput, calls=%fused_computation.24 | convolution fusion | flops 6324224 | bytes 37120 | tf_op jit(solution)/shard_map/dot_general | solution.py:65
  48.0 23.1 %psum.14 = f32[512,16]{1,0:T(8,128)} all-reduce(f32[512,16]{1,0:T(8,128)} %fusion.9), channel_id=1, replica_groups=mesh['sub'=8,'grp'=4] {'grp'}, use_global_device_ids=true, to_apply=%region_0.1 | all-reduce | flops 8192 | bytes 65536 | tf_op jit(solution)/shard_map/psum | solution.py:66
  71.1 26.1 %psum.15 = f32[512,16]{1,0:T(8,128)} all-reduce(f32[512,16]{1,0:T(8,128)} %psum.14), channel_id=1, replica_groups=mesh['sub'=8,'grp'=4] {'sub'}, use_global_device_ids=true, to_apply=%region_1.2 | all-reduce | flops 8192 | bytes 65536 | tf_op jit(solution)/shard_map/psum | solution.py:66
  97.2 1.6 %convolution_bitcast_fusion.2 = f32[128,16]{0,1:T(8,128)S(1)} fusion(f32[512,16]{1,0:T(8,128)} %psum.15, f32[128,512]{1,0:T(8,128)} %param.19), kind=kOutput, calls=%fused_computation.15 | convolution fusion | flops 12582912 | bytes 303104 | tf_op jit(solution)/shard_map/dot_general | solution.py:67
  98.8 13.1 %all_gather.3 = f32[512,16]{0,1:T(8,128)S(1)} all-gather(f32[128,16]{0,1:T(8,128)S(1)} %convolution_bitcast_fusion.2), channel_id=1, replica_groups=mesh['sub'=8,'grp'=4] {'grp'}, dimensions={0}, use_global_device_ids=true | all-gather | bytes 40960 | tf_op jit(solution)/shard_map/all_gather | solution.py:68
  111.9 0.2 fusion.4
  112.1 0.3 convolution_bitcast_fusion
  112.4 2.4 %fusion.3 = bf16[32,16,144]{2,1,0:T(8,128)(2,1)S(1)} fusion(f32[32,16,144]{2,1,0:T(8,128)S(1)} %convolution_bitcast_fusion, bf16[32,144,144]{2,1,0:T(8,128)(2,1)} %param.16, f32[32]{0:T(128)S(1)} %copy-done.6, bf16[32,16,144]{2,1,0:T(8,128)(2,1)S(1)} %copy-done.3), kind=kOutput, calls=%fused_computation.13 | convolution fusion | flops 21676032 | bytes 1917056 | tf_op jit(solution)/shard_map/lrb,lcb->lrc/dot_general | solution.py:75
  114.9 11.9 %all_to_all.22 = bf16[32,16,144]{2,1,0:T(8,128)(2,1)S(1)} all-to-all(bf16[32,16,144]{2,1,0:T(8,128)(2,1)S(1)} %fusion.3), channel_id=1, replica_groups=mesh['sub'=8,'grp'=4] {'sub','grp'}, dimensions={0} | all-to-all | bytes 294912 | tf_op jit(solution)/shard_map/all_to_all | solution.py:8
  126.8 0.3 reshape.72
  127.1 0.3 convolution_convert_fusion
  127.4 0.4 reshape.73
  127.8 12.7 %all_to_all.23 = bf16[32,16,144]{2,1,0:T(8,128)(2,1)S(1)} all-to-all(bf16[32,16,144]{2,1,0:T(8,128)(2,1)S(1)} %reshape.73), channel_id=1, replica_groups=mesh['sub'=8,'grp'=4] {'sub','grp'}, dimensions={0} | all-to-all | bytes 294912 | tf_op jit(solution)/shard_map/all_to_all | solution.py:12
  140.5 0.4 fusion.21
  140.9 0.3 reshape.74
  141.2 0.4 dot_general.66
  141.6 0.9 fusion.7
  142.5 4.7 %convolution_convert_fusion.4 = bf16[64,16,144]{2,1,0:T(8,128)(2,1)} fusion(bf16[64,144,144]{2,1,0:T(8,128)(2,1)} %param.13, f32[64,16,144]{2,0,1:T(8,128)S(1)} %fusion.7, bf16[64,16,144]{2,1,0:T(8,128)(2,1)} %param.11), kind=kOutput, calls=%fused_computation.5 | convolution fusion | flops 43057152 | bytes 3833856 | tf_op jit(solution)/shard_map/erb,ecb->erc/dot_general | solution.py:90
  147.2 0.7 copy.22
  (17 shorter events, 0.0 us)
Async XLA Ops:
  0.6 6.6 %copy-start = (bf16[32,144,144]{2,1,0:T(8,128)(2,1)S(1)}, bf16[32,144,144]{2,1,0:T(8,128)(2,1)}, u32[]{:S(2)}) copy-start(bf16[32,144,144]{2,1,0:T(8,128)(2,1)} %param.14) | copy-start | bytes 3981316
  1.5 5.8 %copy-start.5 = (f32[32]{0:T(128)}, f32[32]{0:T(128)S(1)}, u32[]{:S(2)}) copy-start(f32[32]{0:T(128)S(1)} %fusion.20) | copy-start | bytes 388
  7.3 37.9 %copy-start.1 = (bf16[32,64,144]{2,1,0:T(8,128)(2,1)S(1)}, bf16[32,64,144]{2,1,0:T(8,128)(2,1)}, u32[]{:S(2)}) copy-start(bf16[32,64,144]{2,1,0:T(8,128)(2,1)} %param.17) | copy-start | bytes 1769476
  29.5 82.4 %copy-start.7 = (s32[1,64]{1,0:T(1,128)S(1)}, s32[1,64]{1,0:T(1,128)}, u32[]{:S(2)}) copy-start(s32[1,64]{1,0:T(1,128)} %param.18) | copy-start | bytes 772
  44.5 0.7 copy-start.2
  45.2 67.2 %copy-start.6 = (f32[32]{0:T(128)S(1)}, f32[32]{0:T(128)}, u32[]{:S(2)}) copy-start(f32[32]{0:T(128)} %copy-done.5) | copy-start | bytes 388
  97.2 15.2 %copy-start.3 = (bf16[32,16,144]{2,1,0:T(8,128)(2,1)S(1)}, bf16[32,16,144]{2,1,0:T(8,128)(2,1)}, u32[]{:S(2)}) copy-start(bf16[32,16,144]{2,1,0:T(8,128)(2,1)} %copy-done.2) | copy-start | bytes 442372
  112.4 14.7 %copy-start.4 = (s32[1,32]{1,0:T(1,128)S(1)}, s32[1,32]{1,0:T(1,128)}, u32[]{:S(2)}) copy-start(s32[1,32]{1,0:T(1,128)} %param.20) | copy-start | bytes 388
  140.5 1.1 copy-start.8
